TPU v7x, 32 devices: a whole 2x2x4 slice. The times are simulated.
32 devices in a mesh: row: 4 (over z), col: 8 (over y, x, core).
Axes of the slice: x: 2, y: 2, z: 4, core: 2. Of those that a mesh axis runs over, the one named last changes fastest.
Arguments:
- train_embed: bfloat16 [2048, 256], P(('row', 'col')), may hold values from -16 to 16
- valid_embed: bfloat16 [16384, 256], P(('row', 'col')), may hold values from -16 to 16
- train_labels: int32 [2048], P(('row', 'col')), may hold values from 0 to 99
- valid_labels: int32 [16384], P(('row', 'col')), may hold values from 0 to 99
- pair_level: int32 [100, 100], replicated, may hold values from 0 to 3
- level_cost: float32 [4], replicated, may hold values from 0.05 to 1
Outputs:
- calibrated: float32 [2048], P('row')
All inputs are finite; a program needn't handle non-finite values.
Results may differ from a plain program's by a relative error of at most 0.0003.
Values may be sent and summed in bfloat16 or wider, within the bound.
A program may use at most 64 MiB of HBM per device.

v0:
```python
import math

import jax
import jax.numpy as jnp
from jax import lax
from jax.sharding import PartitionSpec as P

ITERS = 4


entropy_scale = 0.05


def joined(part, axis, combine):
    gathered = jax.tree.map(lambda a: lax.all_gather(a, axis), part)

    def take(source):
        return jax.tree.map(lambda a: lax.dynamic_index_in_dim(a, source, 0, False), gathered)

    return lax.fori_loop(
        1, lax.axis_size(axis), lambda source, state: combine(state, take(source)), take(0)
    )


def inner_products(left_rows, right_rows):
    return lax.dot_general(
        left_rows, right_rows, (((1,), (1,)), ((), ())), preferred_element_type=jnp.float32
    )


def squared_norms(embeddings):
    widened = embeddings.astype(jnp.float32)
    return jnp.sum(widened * widened, axis=1)


def class_costs(pair_level, level_cost):
    num_levels = level_cost.shape[0]
    selected = (
        pair_level[:, :, None] == jnp.arange(num_levels, dtype=jnp.int32)[None, None, :]
    ).astype(jnp.float32)
    return jnp.sum(selected * level_cost[None, None, :], axis=2)


def combine_stats(earlier, later):
    highest = jnp.maximum(earlier[0], later[0])
    return (
        highest,
        earlier[1] * jnp.exp(earlier[0] - highest) + later[1] * jnp.exp(later[0] - highest),
    )


def label_costs(row_labels, class_ids, labels_y):
    col_hot = (class_ids[:, None] == labels_y[None, :]).astype(jnp.float32)
    return jnp.dot(
        row_labels, col_hot, precision=lax.Precision.HIGHEST, preferred_element_type=jnp.float32
    )


def shards(train_embed, valid_embed, train_labels, valid_labels, pair_level, level_cost):
    rows_x, labels_x = (
        lax.all_gather(train_embed, "col", axis=0, tiled=True),
        lax.all_gather(train_labels, "col", axis=0, tiled=True),
    )
    width_d = rows_x.shape[1]
    classes = pair_level.shape[0]
    class_table = class_costs(pair_level, level_cost)
    class_ids = jnp.arange(classes, dtype=jnp.int32)
    train_hot = (labels_x[:, None] == class_ids[None, :]).astype(jnp.float32)
    row_labels = jnp.dot(
        train_hot, class_table, precision=lax.Precision.HIGHEST, preferred_element_type=jnp.float32
    )
    train_sq = squared_norms(rows_x)
    cols_y, labels_y = (
        lax.all_gather(valid_embed, "row", axis=0, tiled=True),
        lax.all_gather(valid_labels, "row", axis=0, tiled=True),
    )
    valid_sq = squared_norms(cols_y)
    label_full = label_costs(row_labels, class_ids, labels_y)

    def cost_block(offset, block_cols):
        block_y = lax.dynamic_slice_in_dim(cols_y, offset, block_cols, 0)
        block_sq = lax.dynamic_slice_in_dim(valid_sq, offset, block_cols, 0)
        label_slice = lax.dynamic_slice_in_dim(label_full, offset, block_cols, 1)
        return (
            train_sq[:, None] + block_sq[None, :] - 2.0 * inner_products(rows_x, block_y)
        ) / width_d + label_slice

    row_count = rows_x.shape[0]
    col_count = labels_y.shape[0]
    block_cols = min(512, col_count)
    block_count = col_count // block_cols
    block_ids = jnp.arange(block_count, dtype=jnp.int32)

    def scores(block_index, row_pot, col_pot):
        offset = block_index * block_cols
        cost_tile = cost_block(offset, block_cols)
        block_pot = lax.dynamic_slice_in_dim(col_pot, offset, block_cols, 0)
        return (
            (block_pot[None, :] - cost_tile) / entropy_scale,
            (row_pot[:, None] - cost_tile) / entropy_scale,
        )

    row_pot = jnp.zeros((row_count,), jnp.float32)
    col_pot = jnp.zeros((col_count,), jnp.float32)
    full_rows = row_count * lax.axis_size("row")
    full_cols = col_count * lax.axis_size("col")
    for iteration in range(ITERS):

        def visit(running, block_index, row_pot=row_pot, col_pot=col_pot):
            row_side, col_side = scores(block_index, row_pot, col_pot)
            highest = jnp.maximum(running[0], jnp.max(row_side, axis=1))
            summed = running[1] * jnp.exp(running[0] - highest) + jnp.sum(
                jnp.exp(row_side - highest[:, None]), axis=1
            )
            col_high = jnp.max(col_side, axis=0)
            col_summed = jnp.sum(jnp.exp(col_side - col_high[None, :]), axis=0)
            return ((highest, summed), (col_high, col_summed))

        start_state = (
            jnp.full((row_count,), -jnp.inf, jnp.float32),
            jnp.zeros((row_count,), jnp.float32),
        )
        row_state, col_state = lax.scan(visit, start_state, block_ids)
        row_high, row_sum = joined(row_state, "col", combine_stats)
        col_high, col_sum = joined(
            (col_state[0].reshape(col_count), col_state[1].reshape(col_count)), "row", combine_stats
        )
        row_new = entropy_scale * math.log(full_cols) - entropy_scale * (
            row_high + jnp.log(row_sum)
        )
        col_new = entropy_scale * math.log(full_rows) - entropy_scale * (
            col_high + jnp.log(col_sum)
        )
        row_pot = 0.5 * (row_pot + row_new)
        col_pot = 0.5 * (col_pot + col_new)
    potential_sum = lax.psum(jnp.sum(row_pot), "row")
    return (row_pot * full_rows - potential_sum) / (full_rows - 1)


def solution(mesh):
    placed = (
        P(("row", "col"), None),
        P(("row", "col"), None),
        P(("row", "col")),
        P(("row", "col")),
        P(),
        P(),
    )
    return jax.shard_map(shards, mesh=mesh, in_specs=placed, out_specs=P("row"), check_vma=False)
```

profile of v0, /device:TPU:0, one launch (start us, length us, event | category | flops | bytes accessed | tf_op | source)
XLA Modules:
  0.0 279.1 jit_solution(14730192426939712752)
XLA Ops:
  10.2 9.5 %all-reduce = s32[512]{0:T(512)S(1)} all-reduce(s32[512]{0:T(512)S(1)} %dynamic-update-slice), channel_id=1, replica_groups=mesh['row'=4,'col'=8] {'col'}, use_global_device_ids=true, to_apply=%add | all-reduce | flops 512 | bytes 4096
  19.7 12.7 %all-gather.8 = s32[4,1,512]{2,1,0:T(1,128)S(1)} all-gather(s32[1,1,512]{2,1,0:T(1,128)} %bitcast.250), channel_id=1, replica_groups=mesh['row'=4,'col'=8] {'row'}, dimensions={0}, use_global_device_ids=true | all-gather | bytes 10240 | tf_op jit(solution)/shard_map/all_gather | solution.py:75
  32.4 8.7 %all_gather.78 = bf16[512,256]{1,0:T(8,128)(2,1)S(1)} all-gather(bf16[64,256]{1,0:T(8,128)(2,1)} %param.28), channel_id=1, replica_groups=mesh['row'=4,'col'=8] {'col'}, dimensions={0}, use_global_device_ids=true | all-gather | bytes 294912 | tf_op jit(solution)/shard_map/all_gather | solution.py:61
  42.6 3.8 %fusion.36 = f32[512,2048]{0,1:T(8,128)} fusion(f32[512,100]{0,1:T(8,128)S(1)} %fusion.38, s32[2048]{0:T(1024)S(1)} %bitcast.249), kind=kOutput, calls=%fused_computation.82 | convolution fusion | flops 1258496000 | bytes 4407296 | tf_op jit(solution)/shard_map/dot_general | solution.py:54
  48.0 14.7 %while.190 = (s32[]{:T(128)}, f32[512]{0:T(512)S(1)}, f32[512]{0:T(512)S(1)}, f32[4,512]{1,0:T(4,128)S(1)}, f32[4,512]{1,0:T(4,128)S(1)}, /*index=5*/f32[512]{0:...) while((s32[]{:T(128)}, f32[512]{0:T(512)S(1)}, ...), condition=%wide.region_8.9_spmd.clone, body=%wide.region_3.8_spmd.clone.sunk | while | flops 137627136 | bytes 3720414 | solution.py:123
  49.3 1.9 fusion.61
  62.8 8.5 %all-gather.9 = f32[8,1,512]{2,1,0:T(1,128)S(1)} all-gather(f32[1,1,512]{2,1,0:T(1,128)S(1)} %bitcast.208), channel_id=2, replica_groups=mesh['row'=4,'col'=8] {'col'}, dimensions={0}, use_global_device_ids=true | all-gather | bytes 18432 | tf_op jit(solution)/shard_map/all_gather | solution.py:15
  71.3 8.3 %all-gather.10 = f32[8,1,512]{2,1,0:T(1,128)S(1)} all-gather(f32[1,1,512]{2,1,0:T(1,128)S(1)} %bitcast.240), channel_id=3, replica_groups=mesh['row'=4,'col'=8] {'col'}, dimensions={0}, use_global_device_ids=true | all-gather | bytes 18432 | tf_op jit(solution)/shard_map/all_gather | solution.py:15
  79.6 13.1 %all-gather.11 = f32[4,1,2048]{2,1,0:T(1,128)S(1)} all-gather(f32[1,1,2048]{2,1,0:T(1,128)S(1)} %reshape.65), channel_id=1, replica_groups=mesh['row'=4,'col'=8] {'row'}, dimensions={0}, use_global_device_ids=true | all-gather | bytes 40960 | tf_op jit(solution)/shard_map/all_gather | solution.py:15
  92.8 13.1 %all-gather.12 = f32[4,1,2048]{2,1,0:T(1,128)S(1)} all-gather(f32[1,1,2048]{2,1,0:T(1,128)S(1)} %reshape.67), channel_id=1, replica_groups=mesh['row'=4,'col'=8] {'row'}, dimensions={0}, use_global_device_ids=true | all-gather | bytes 40960 | tf_op jit(solution)/shard_map/all_gather | solution.py:15
  106.7 16.9 %while.191 = (s32[]{:T(128)}, f32[512]{0:T(512)S(1)}, f32[512]{0:T(512)S(1)}, f32[4,512]{1,0:T(4,128)S(1)}, f32[4,512]{1,0:T(4,128)S(1)}, /*index=5*/s32[4]{0:T(...) while((s32[]{:T(128)}, f32[512]{0:T(512)S(1)}, ...), condition=%wide.region_18.19_spmd.clone, body=%wide.region_13.18_spmd.clone.sunk | while | flops 139200000 | bytes 3732722 | solution.py:123
  108.2 2.0 fusion.64
  112.4 2.0 fusion.64
  116.6 2.0 fusion.64
  120.9 2.0 fusion.64
  123.6 8.5 %all-gather.13 = f32[8,1,512]{2,1,0:T(1,128)S(1)} all-gather(f32[1,1,512]{2,1,0:T(1,128)S(1)} %bitcast.207), channel_id=4, replica_groups=mesh['row'=4,'col'=8] {'col'}, dimensions={0}, use_global_device_ids=true | all-gather | bytes 18432 | tf_op jit(solution)/shard_map/all_gather | solution.py:15
  132.1 8.3 %all-gather.14 = f32[8,1,512]{2,1,0:T(1,128)S(1)} all-gather(f32[1,1,512]{2,1,0:T(1,128)S(1)} %bitcast.239), channel_id=5, replica_groups=mesh['row'=4,'col'=8] {'col'}, dimensions={0}, use_global_device_ids=true | all-gather | bytes 18432 | tf_op jit(solution)/shard_map/all_gather | solution.py:15
  140.4 13.1 %all-gather.15 = f32[4,1,2048]{2,1,0:T(1,128)S(1)} all-gather(f32[1,1,2048]{2,1,0:T(1,128)S(1)} %reshape.73), channel_id=1, replica_groups=mesh['row'=4,'col'=8] {'row'}, dimensions={0}, use_global_device_ids=true | all-gather | bytes 40960 | tf_op jit(solution)/shard_map/all_gather | solution.py:15
  153.6 13.1 %all-gather.16 = f32[4,1,2048]{2,1,0:T(1,128)S(1)} all-gather(f32[1,1,2048]{2,1,0:T(1,128)S(1)} %reshape.75), channel_id=1, replica_groups=mesh['row'=4,'col'=8] {'row'}, dimensions={0}, use_global_device_ids=true | all-gather | bytes 40960 | tf_op jit(solution)/shard_map/all_gather | solution.py:15
  167.5 16.4 %while.192 = (s32[]{:T(128)}, f32[512]{0:T(512)S(1)}, f32[512]{0:T(512)S(1)}, f32[4,512]{1,0:T(4,128)S(1)}, f32[4,512]{1,0:T(4,128)S(1)}, /*index=5*/s32[4]{0:T(...) while((s32[]{:T(128)}, f32[512]{0:T(512)S(1)}, ...), condition=%wide.region_28.29_spmd.clone, body=%wide.region_23.28_spmd.clone.sunk | while | flops 139200000 | bytes 3732722 | solution.py:123
  168.9 2.0 fusion.67
  173.0 2.0 fusion.67
  177.1 2.0 fusion.67
  181.2 2.0 fusion.67
  183.9 8.5 %all-gather.17 = f32[8,1,512]{2,1,0:T(1,128)S(1)} all-gather(f32[1,1,512]{2,1,0:T(1,128)S(1)} %bitcast.206), channel_id=6, replica_groups=mesh['row'=4,'col'=8] {'col'}, dimensions={0}, use_global_device_ids=true | all-gather | bytes 18432 | tf_op jit(solution)/shard_map/all_gather | solution.py:15
  192.4 8.3 %all-gather.18 = f32[8,1,512]{2,1,0:T(1,128)S(1)} all-gather(f32[1,1,512]{2,1,0:T(1,128)S(1)} %bitcast.238), channel_id=7, replica_groups=mesh['row'=4,'col'=8] {'col'}, dimensions={0}, use_global_device_ids=true | all-gather | bytes 18432 | tf_op jit(solution)/shard_map/all_gather | solution.py:15
  200.7 13.1 %all-gather.19 = f32[4,1,2048]{2,1,0:T(1,128)S(1)} all-gather(f32[1,1,2048]{2,1,0:T(1,128)S(1)} %reshape.81), channel_id=1, replica_groups=mesh['row'=4,'col'=8] {'row'}, dimensions={0}, use_global_device_ids=true | all-gather | bytes 40960 | tf_op jit(solution)/shard_map/all_gather | solution.py:15
  213.9 13.1 %all-gather.20 = f32[4,1,2048]{2,1,0:T(1,128)S(1)} all-gather(f32[1,1,2048]{2,1,0:T(1,128)S(1)} %reshape.83), channel_id=1, replica_groups=mesh['row'=4,'col'=8] {'row'}, dimensions={0}, use_global_device_ids=true | all-gather | bytes 40960 | tf_op jit(solution)/shard_map/all_gather | solution.py:15
  227.3 14.3 %while.193 = (s32[]{:T(128)}, f32[512]{0:T(512)S(1)}, f32[512]{0:T(512)S(1)}, s32[4]{0:T(128)S(1)}, f32[2048]{0:T(1024)S(1)}, /*index=5*/f32[512]{0:T(512)S(1)},...) while((s32[]{:T(128)}, f32[512]{0:T(512)S(1)}, ...), condition=%wide.region_36.37_spmd.clone, body=%wide.region_33.36_spmd.clone.sunk | while | flops 136841728 | bytes 3712210 | solution.py:123
  241.6 8.5 %all-gather.21 = f32[8,1,512]{2,1,0:T(1,128)S(1)} all-gather(f32[1,1,512]{2,1,0:T(1,128)S(1)} %bitcast.205), channel_id=8, replica_groups=mesh['row'=4,'col'=8] {'col'}, dimensions={0}, use_global_device_ids=true | all-gather | bytes 18432 | tf_op jit(solution)/shard_map/all_gather | solution.py:15
  250.2 8.3 %all-gather.22 = f32[8,1,512]{2,1,0:T(1,128)S(1)} all-gather(f32[1,1,512]{2,1,0:T(1,128)S(1)} %bitcast.237), channel_id=9, replica_groups=mesh['row'=4,'col'=8] {'col'}, dimensions={0}, use_global_device_ids=true | all-gather | bytes 18432 | tf_op jit(solution)/shard_map/all_gather | solution.py:15
  259.9 11.1 %psum.7 = f32[]{:T(128)} all-reduce(f32[]{:T(128)} %get-tuple-element.1701), channel_id=1, replica_groups=mesh['row'=4,'col'=8] {'row'}, use_global_device_ids=true, to_apply=%region_40.41 | all-reduce | flops 1 | bytes 8 | tf_op jit(solution)/shard_map/psum | solution.py:136
  (289 shorter events, 45.2 us)
Async XLA Ops:
  6.5 39.9 %all-gather.25.cloned.1.call-start = ((), (), s32[]{:S(2)}) async-start(), calls=%async_computation | async-start | bytes 1310720 | tf_op jit(solution)/shard_map/all_gather | solution.py:74
Sparse Core Ops, SparseCore 0:
  8.9 30.8 all-gather.24
where the time goes:
time: 280 us; the launch traced here: 279 us
  blocking collectives  188 us (67%)
  matrix products  34.7 us (12%)
  local copies, waits for them, and re-layouts  16.4 us (6%)
  between operations  14.5 us (5%)
  other arithmetic  12.7 us (5%)
  loops' own time  12.1 us (4%)
    all_gather x14, blocking collectives, joined(): gathered = jax.tree.map(lambda a: lax.all_gather(a, axis), part)  146 us
    dot_general x16, matrix products, inner_products(): lax.dot_general(left_rows, right_rows, (((1,), (1,)), ((), ())), preferre...  30.5 us
    all_gather x1, blocking collectives, shards(): lax.all_gather(valid_labels, 'row', axis=0, tiled=True)  12.7 us
    psum x1, blocking collectives, shards(): potential_sum = lax.psum(jnp.sum(row_pot), 'row')  11.1 us
    another operation x4, loops' own time, shards(): row_state, col_state = lax.scan(visit, start_state, block_ids)  11 us
    dynamic_slice x16, local copies, waits for them, and re-layouts, shards(): row_state, col_state = lax.scan(visit, start_state, block_ids)  10.1 us
    unnamed x1, blocking collectives  9.49 us
    all_gather x1, blocking collectives, shards(): lax.all_gather(train_embed, 'col', axis=0, tiled=True)  8.67 us
  transfers between devices with their start and end apart: 1, of which 0 were waited for; matrix products, arithmetic and copies ran while one was open for 3% of the time, Pallas kernels for 0%

commit v1 on v0

v1 whole, which is shorter than its diff:
```python
import functools
import math

import jax
import jax.numpy as jnp
from jax import lax
from jax.experimental import pallas as pl
from jax.experimental.pallas import tpu as pltpu
from jax.sharding import PartitionSpec as P

ITERS = 4
entropy_scale = 0.05
SCALE = math.log2(math.e) / entropy_scale
LOG2E = math.log2(math.e)
NT = (((1,), (1,)), ((), ()))
LANES = 128


def log2(x):
    return jnp.log(x) * LOG2E


def pieces(x, count):
    out = []
    for _ in range(count):
        part = x.astype(jnp.bfloat16)
        out.append(part)
        x = x - part.astype(jnp.float32)
    return out


def dot(a, b, dims=(((1,), (0,)), ((), ()))):
    return lax.dot_general(a, b, dims, preferred_element_type=jnp.float32)


def kernel(nr, nc, n, level_ref, pair_ref, block_ref, valid_ref, vlab_ref, out_ref,
           buf, cost, y_ref, b_ref, a_ref, norm_ref, table_ref, pbuf, zbuf,
           local_sem, gsend1, gsend2, gsend3, grecv, psend, precv, zsend, zrecv):
    width = valid_ref.shape[1]
    nv = valid_ref.shape[0]
    nt = nr * nc * n
    nh = nc // 2
    kap = SCALE / width
    r = lax.axis_index("row")
    c = lax.axis_index("col")
    hi = c // 2
    lo = c % 2
    partner = hi * 2 + (1 - lo)
    me = r * nc + c

    def rc(src, dst, ss, rs, row, col):
        return pltpu.make_async_remote_copy(
            src_ref=src, dst_ref=dst, send_sem=ss, recv_sem=rs,
            device_id={"row": row, "col": col}, device_id_type=pl.DeviceIdType.MESH)

    def loop(lower, upper, body):
        if upper - lower <= 8:
            for i in range(lower, upper):
                body(i)
        else:
            lax.fori_loop(lower, upper, lambda i, _: (body(i), 0)[1], 0)

    barrier = pltpu.get_barrier_semaphore()
    loop(1, nr, lambda d: pl.semaphore_signal(
        barrier, inc=1, device_id={"row": (r + d) % nr, "col": c}, device_id_type=pl.DeviceIdType.MESH))
    loop(1, nc, lambda d: pl.semaphore_signal(
        barrier, inc=1, device_id={"row": r, "col": (c + d) % nc}, device_id_type=pl.DeviceIdType.MESH))
    own = pltpu.make_async_copy(block_ref, buf.at[me], local_sem)
    own.start()
    pl.semaphore_wait(barrier, nr + nc - 2)

    def to_row(d):
        return rc(block_ref, buf.at[me], gsend1.at[d], grecv.at[me], (r + d) % nr, c)

    def to_plane(src, b, dr, d):
        return rc(src, buf.at[b], gsend2.at[dr, d], grecv.at[b], r, ((hi + d) % nh) * 2 + lo)

    def to_partner(src, b, k):
        return rc(src, buf.at[b], gsend3.at[k], grecv.at[b], r, partner)

    def arrived(b):
        rc(buf.at[b], buf.at[b], local_sem, grecv.at[b], r, partner).wait_recv()

    loop(1, nr, lambda d: to_row(d).start())
    loop(1, nh, lambda d: to_plane(block_ref, me, 0, d).start())
    to_partner(block_ref, me, 0).start()

    valid = valid_ref[...]
    wide = valid.astype(jnp.float32)
    b_ref[...] = jnp.broadcast_to(-kap * jnp.sum(wide * wide, axis=1, keepdims=True), b_ref.shape)
    classes = pair_ref.shape[0]
    pair = pair_ref[...]
    table = jnp.zeros(pair.shape, jnp.float32)
    for level in range(level_ref.shape[0]):
        table = table + jnp.where(pair == level, level_ref[level], 0.0)
    table_ref[...] = jnp.zeros_like(table_ref)
    table_ref[0:classes, 0:classes] = table * (-0.5 * width)
    hot = (lax.broadcasted_iota(jnp.int32, (LANES, nv), 0) == vlab_ref[...]).astype(jnp.float32)
    hot = hot.T.astype(jnp.bfloat16)
    for k, part in enumerate(pieces(table_ref[...], 3)):
        y_ref[k] = dot(hot, part, NT).astype(jnp.bfloat16)

    def forward_row(d):
        b = ((r + nr - d) % nr) * nc + c
        arrived(b)
        loop(1, nh, lambda e: to_plane(buf.at[b], b, d, e).start())
        to_partner(buf.at[b], b, d * nh).start()

    loop(1, nr, forward_row)

    def forward_plane(d):
        def one(e):
            b = ((r + nr - d) % nr) * nc + ((hi + nh - e) % nh) * 2 + lo
            arrived(b)
            to_partner(buf.at[b], b, d * nh + e).start()
        loop(1, nh, one)

    loop(0, nr, forward_plane)
    loop(0, nr, lambda d: loop(0, nh, lambda e: arrived(
        ((r + nr - d) % nr) * nc + ((hi + nh - e) % nh) * 2 + (1 - lo))))
    own.wait()

    chunk = 256
    per = chunk // n
    ones = jnp.ones((8, width), jnp.bfloat16)

    def build(m, _):
        rows = buf[pl.ds(m * per, per), 0:n, :].reshape(chunk, width)
        lane = lax.broadcasted_iota(jnp.int32, (1, chunk), 1) // n
        labels = jnp.zeros((1, chunk), jnp.float32)
        for q in range(per):
            extra = buf[m * per + q, n:n + 16, :].astype(jnp.float32)
            labels = jnp.where(lane == q, extra[0:1, 0:chunk], labels)
        ids = lax.broadcasted_iota(jnp.int32, (LANES, chunk), 0)
        t_hot = (ids == labels.astype(jnp.int32)).astype(jnp.float32).astype(jnp.bfloat16)
        total = dot(valid_ref[...], rows, NT)
        for k in range(3):
            total = total + dot(y_ref[k], t_hot)
        at = pl.ds(pl.multiple_of(m * chunk, chunk), chunk)
        cost[:, at] = total * (2.0 * kap)
        wide = rows.astype(jnp.float32)
        high, low = pieces(wide * wide, 2)
        sq = dot(ones, high, NT) + dot(ones, low, NT)
        norm_ref[:, at] = sq[0:1] * kap
        return 0

    lax.fori_loop(0, nt // chunk, build, 0)
    a_ref[0] = -norm_ref[...]

    full_rows = nt
    full_cols = nv * nr * nc
    span = 512

    def row_side(e):
        for w in range(nt // span):
            at = slice(w * span, (w + 1) * span)

            def term(k):
                rows = pl.ds(pl.multiple_of(k * 8, 8), 8)
                pot = b_ref[rows, :]
                return cost[rows, at] + jnp.concatenate([pot] * (span // LANES), axis=1)

            high = lax.fori_loop(0, nv // 8, lambda k, h: jnp.maximum(h, term(k)),
                                 jnp.full((8, span), -jnp.inf, jnp.float32), unroll=8)
            high = jnp.max(high, axis=0, keepdims=True)
            wide_high = jnp.broadcast_to(high, (8, span))
            total = lax.fori_loop(0, nv // 8, lambda k, s: s + jnp.exp2(term(k) - wide_high),
                                  jnp.zeros((8, span), jnp.float32), unroll=8)
            total = jnp.sum(total, axis=0, keepdims=True)
            pbuf[e, c, :, at] = high + log2(total)

    def col_side(a):
        pot = jnp.broadcast_to(a, (8, nt))

        def one(k, _):
            rows = pl.ds(pl.multiple_of(k * 8, 8), 8)
            t = cost[rows, :] + pot
            high = jnp.max(t, axis=1, keepdims=True)
            total = jnp.sum(jnp.exp2(t - high), axis=1, keepdims=True)
            new = math.log2(full_rows) - (high + log2(total))
            b_ref[rows, :] = 0.5 * (b_ref[rows, :] + new)
            return 0

        lax.fori_loop(0, nv // 8, one, 0, unroll=4)

    def p_copy(e, d, to):
        src = c if to else (c + nc - d) % nc
        return rc(pbuf.at[e, src], pbuf.at[e, src], psend.at[e, d], precv.at[e, d], r, (c + d) % nc)

    def z_copy(e, d, to):
        src = r if to else (r + nr - d) % nr
        return rc(zbuf.at[e, src], zbuf.at[e, src], zsend.at[e, d], zrecv.at[e, d], (r + d) % nr, c)

    def joined(parts):
        high = jnp.max(parts, axis=0)
        return high + log2(jnp.sum(jnp.exp2(parts - high[None]), axis=0))

    def send_plane(e):
        loop(1, nc, lambda d: p_copy(e, d, True).start())

    def turn(e):
        loop(1, nc, lambda d: p_copy(e, d, False).wait_recv())
        zbuf[e, r] = joined(pbuf[e])
        loop(1, nr, lambda d: z_copy(e, d, True).start())

    def finish(e):
        loop(1, nr, lambda d: z_copy(e, d, False).wait_recv())
        a_ref[e + 1] = 0.5 * (a_ref[e] + (math.log2(full_cols) - joined(zbuf[e])))

    row_side(0)
    send_plane(0)
    col_side(a_ref[0])
    row_side(1)
    send_plane(1)
    for e in range(0, ITERS, 2):
        turn(e)
        turn(e + 1)
        finish(e)
        if e + 2 < ITERS:
            col_side(a_ref[e + 1])
            row_side(e + 2)
            send_plane(e + 2)
        finish(e + 1)
        if e + 3 < ITERS:
            col_side(a_ref[e + 2])
            row_side(e + 3)
            send_plane(e + 3)

    row_pot = (a_ref[ITERS] + norm_ref[...]) * (1.0 / SCALE)
    result = (row_pot * full_rows - jnp.sum(row_pot, axis=1, keepdims=True)) * (1.0 / (full_rows - 1))
    norm_ref[...] = result
    span_out = nt // nr
    out_ref[...] = norm_ref[:, pl.ds(pl.multiple_of(r * span_out, span_out), span_out)]

    loop(1, nr, lambda d: to_row(d).wait_send())
    loop(0, nr, lambda d: loop(1, nh, lambda e: to_plane(block_ref, me, d, e).wait_send()))
    loop(0, nr, lambda d: loop(0, nh, lambda e: to_partner(block_ref, me, d * nh + e).wait_send()))
    for e in range(ITERS):
        loop(1, nc, lambda d: p_copy(e, d, True).wait_send())
        loop(1, nr, lambda d: z_copy(e, d, True).wait_send())


def solution(mesh):
    nr, nc = mesh.shape["row"], mesh.shape["col"]

    def shards(train_embed, valid_embed, train_labels, valid_labels, pair_level, level_cost):
        n, width = train_embed.shape
        nv = valid_embed.shape[0]
        nt = nr * nc * n
        labels = jnp.tile(train_labels.astype(jnp.bfloat16), width // n)[None, :]
        block = jnp.concatenate([train_embed, jnp.broadcast_to(labels, (16, width))], axis=0)
        vmem = pl.BlockSpec(memory_space=pltpu.VMEM)
        dma = pltpu.SemaphoreType.DMA
        out = pl.pallas_call(
            functools.partial(kernel, nr, nc, n),
            out_shape=jax.ShapeDtypeStruct((1, nt // nr), jnp.float32),
            in_specs=[pl.BlockSpec(memory_space=pltpu.SMEM)] + [vmem] * 4,
            out_specs=vmem,
            scratch_shapes=[
                pltpu.VMEM((nr * nc, n + 16, width), jnp.bfloat16),
                pltpu.VMEM((nv, nt), jnp.float32),
                pltpu.VMEM((3, nv, LANES), jnp.bfloat16),
                pltpu.VMEM((nv, LANES), jnp.float32),
                pltpu.VMEM((ITERS + 1, 1, nt), jnp.float32),
                pltpu.VMEM((1, nt), jnp.float32),
                pltpu.VMEM((LANES, LANES), jnp.float32),
                pltpu.VMEM((ITERS, nc, 1, nt), jnp.float32),
                pltpu.VMEM((ITERS, nr, 1, nt), jnp.float32),
                dma, dma((nr,)), dma((nr, nc // 2)), dma((nr * (nc // 2),)), dma((nr * nc,)),
                dma((ITERS, nc)), dma((ITERS, nc)), dma((ITERS, nr)), dma((ITERS, nr)),
            ],
            compiler_params=pltpu.CompilerParams(
                collective_id=0, has_side_effects=True, vmem_limit_bytes=56 * 1024 * 1024),
            name="sinkhorn",
        )(level_cost, pair_level, block, valid_embed, valid_labels[None, :])
        return out.reshape(nt // nr)

    placed = (
        P(("row", "col"), None),
        P(("row", "col"), None),
        P(("row", "col")),
        P(("row", "col")),
        P(),
        P(),
    )
    return jax.shard_map(shards, mesh=mesh, in_specs=placed, out_specs=P("row"), check_vma=False)
```

time: 280 us -> 54.3 us (0.19)
  blocking collectives: 188 us -> 0 us
  Pallas kernels: 0 us -> 50.7 us
  matrix products: 34.7 us -> 0 us
  between operations: 14.5 us -> 0.01 us
  local copies, waits for them, and re-layouts: 16.4 us -> 1.99 us
  loops' own time: 12.1 us -> 0 us
  other arithmetic: 12.7 us -> 1.38 us
    all_gather x16 -> x0, blocking collectives: 168 us -> none  [the longest x14 146 us: joined(): gathered = jax.tree.map(lambda a: lax.all_gather(a, axis), part)]
    pallas_call x0 -> x1, Pallas kernels: none -> 50.7 us  [shards(): pl.pallas_call(functools.partial(kernel, nr, nc, n), out_shape=jax.ShapeD...]
    dot_general x18 -> x0, matrix products: 34.7 us -> none  [the longest x16 30.5 us: inner_products(): lax.dot_general(left_rows, right_rows, (((1,), (1,)), ((), ())), preferre...]
    dynamic_slice x95 -> x0, local copies, waits for them, and re-layouts: 12.8 us -> none  [the longest x16 10.1 us: shards(): row_state, col_state = lax.scan(visit, start_state, block_ids)]
    another operation x11 -> x0, loops' own time: 12.1 us -> none  [the longest x4 11 us: shards(): row_state, col_state = lax.scan(visit, start_state, block_ids)]
    psum x1 -> x0, blocking collectives: 11.1 us -> none  [shards(): potential_sum = lax.psum(jnp.sum(row_pot), 'row')]
    reduce_sum x20 -> x0, other arithmetic: 10.3 us -> none  [the longest x12 6.09 us: visit(): col_summed = jnp.sum(jnp.exp(col_side - col_high[None, :]), axis=0)]
    unnamed x1 -> x0, blocking collectives: 9.49 us -> none
  transfers between devices with their start and end apart: 1 -> 0, of which waited for: 0 -> 0; matrix products, arithmetic and copies ran while one was open for 3% -> 0% of each run, Pallas kernels for 0% -> 0%
where the time goes in v1:
time: 54.3 us; the launch traced here: 54 us
  Pallas kernels  50.7 us (93%)
  local copies, waits for them, and re-layouts  1.99 us (4%)
  other arithmetic  1.38 us (3%)
    pallas_call x1, Pallas kernels, shards(): pl.pallas_call(functools.partial(kernel, nr, nc, n), out_shape=jax.ShapeD...  50.7 us
    unnamed x3, local copies, waits for them, and re-layouts  1.89 us
    concatenate x1, other arithmetic, shards(): jnp.concatenate([train_embed, jnp.broadcast_to(labels, (16, width))], axi...  1.38 us

profile of v1, /device:TPU:0, one launch (start us, length us, event | category | flops | bytes accessed | tf_op | source)
XLA Modules:
  0.0 54.0 jit_solution(10429202629284592421)
XLA Ops:
  0.0 0.0 copy-start
  0.0 0.7 %copy-done = s32[64]{0:T(128)S(1)} copy-done((s32[64]{0:T(128)S(1)}, s32[64]{0:T(128)}, u32[]{:S(2)}) %copy-start) | copy-done | bytes 280
  0.7 0.1 broadcast_in_dim.10
  0.8 1.4 %pad_maximum_fusion.block_ref = bf16[80,256]{1,0:T(8,128)(2,1)} fusion(bf16[16,256]{1,0:T(8,128)(2,1)S(1)} %broadcast_in_dim.11, bf16[64,256]{1,0:T(8,128)(2,1)} %param.6), kind=kLoop, calls=%fused_computation | loop fusion | flops 81920 | bytes 81920 | tf_op jit(solution)/shard_map/concatenate | solution.py:251
  2.1 50.7 %sinkhorn.1 = f32[1,512]{1,0:T(1,128)} custom-call(f32[4]{0:T(128)} %level_ref.1, s32[100,100]{1,0:T(8,128)} %pair_ref.1, bf16[80,256]{1,0:T(8,128)(2,1)} %pad_maximum_fusion.block_ref, bf16[512,256]{1,0:T(8,128)(2,1)} %valid_ref.1, s32[1,512]{1,0:T(1,128)} %bitcast.3), custom_call_target="tpu_custom_call" | custom-call | tf_op jit(solution)/shard_map/sinkhorn/pallas_call | solution.py:254
  52.8 1.2 %copy.8 = f32[512]{0:T(512)} copy(f32[512]{0:T(512)} %bitcast.2) | data formatting | bytes 4096
  (3 shorter events, 0.0 us)
Async XLA Ops:
  0.0 0.7 %copy-start = (s32[64]{0:T(128)S(1)}, s32[64]{0:T(128)}, u32[]{:S(2)}) copy-start(s32[64]{0:T(128)} %param.8) | copy-start | bytes 772

commit v2 on v1

v2 whole, which is shorter than its diff:
```python
import functools
import math

import jax
import jax.numpy as jnp
from jax import lax
from jax.experimental import pallas as pl
from jax.experimental.pallas import tpu as pltpu
from jax.sharding import PartitionSpec as P

ITERS = 4
entropy_scale = 0.05
SCALE = math.log2(math.e) / entropy_scale
LOG2E = math.log2(math.e)
NT = (((1,), (1,)), ((), ()))
LANES = 128


def log2(x):
    return jnp.log(x) * LOG2E


def pieces(x, count):
    out = []
    for _ in range(count):
        part = x.astype(jnp.bfloat16)
        out.append(part)
        x = x - part.astype(jnp.float32)
    return out


def dot(a, b, dims=(((1,), (0,)), ((), ()))):
    return lax.dot_general(a, b, dims, preferred_element_type=jnp.float32)


def kernel(nr, nc, n, level_hbm, pair_hbm, block_ref, lab_ref, valid_hbm, vlab_hbm, out_ref,
           buf, labs, level_ref, pair_ref, valid_ref, vlab_ref,
           cost, y_ref, b_ref, a_ref, norm_ref, table_ref, part_ref, high_ref, pbuf, zbuf,
           local_sem, gsend, lsend, grecv, lrecv, psend, precv, zsend, zrecv):
    width = valid_ref.shape[1]
    nv = valid_ref.shape[0]
    nt = nr * nc * n
    nh = nc // 2
    kap = SCALE / width
    r = lax.axis_index("row")
    c = lax.axis_index("col")
    hi = c // 2
    lo = c % 2
    me = r * nc + c

    def rc(src, dst, ss, rs, row, col):
        return pltpu.make_async_remote_copy(
            src_ref=src, dst_ref=dst, send_sem=ss, recv_sem=rs,
            device_id={"row": row, "col": col}, device_id_type=pl.DeviceIdType.MESH)

    def loop(lower, upper, body):
        if upper - lower <= 8:
            for i in range(lower, upper):
                body(i)
        else:
            lax.fori_loop(lower, upper, lambda i, _: (body(i), 0)[1], 0)

    pairs = ((level_hbm, level_ref), (pair_hbm, pair_ref), (valid_hbm, valid_ref), (vlab_hbm, vlab_ref),
             (block_ref, buf.at[me]), (lab_ref, labs.at[me]))
    copies = [pltpu.make_async_copy(src, dst, local_sem.at[k]) for k, (src, dst) in enumerate(pairs)]
    for copy in copies:
        copy.start()

    barrier = pltpu.get_barrier_semaphore()
    loop(1, nr, lambda d: pl.semaphore_signal(
        barrier, inc=1, device_id={"row": (r + d) % nr, "col": c}, device_id_type=pl.DeviceIdType.MESH))
    loop(1, nc, lambda d: pl.semaphore_signal(
        barrier, inc=1, device_id={"row": r, "col": (c + d) % nc}, device_id_type=pl.DeviceIdType.MESH))
    pl.semaphore_wait(barrier, nr + nc - 2)

    square = nr == 4
    quad = nh == 4

    def flip(x, k):
        if k == 1:
            return x + 1 - 2 * (x % 2)
        return (x + 2) % 4 if k == 2 else 3 - x

    def row_to(d):
        return (flip(r, d) if d else r) if square else (r + d) % nr

    def row_from(d):
        return (flip(r, d) if d else r) if square else (r + nr - d) % nr

    def send(b, k, row, col, own):
        data = rc(block_ref if own else buf.at[b], buf.at[b], gsend.at[k], grecv.at[b], row, col)
        label = rc(lab_ref if own else labs.at[b], labs.at[b], lsend.at[k], lrecv.at[b], row, col)
        data.start()
        label.start()

    def sent(k):
        rc(block_ref, buf.at[me], gsend.at[k], grecv.at[me], r, hi * 2 + 1 - lo).wait_send()
        rc(lab_ref, labs.at[me], lsend.at[k], lrecv.at[me], r, hi * 2 + 1 - lo).wait_send()

    def arrived(b):
        rc(buf.at[b], buf.at[b], gsend.at[0], grecv.at[b], r, hi * 2 + 1 - lo).wait_recv()
        rc(labs.at[b], labs.at[b], lsend.at[0], lrecv.at[b], r, hi * 2 + 1 - lo).wait_recv()

    def block_id(d, high):
        return row_from(d) * nc + high * 2 + lo

    def to_plane(b, d, own):
        if quad:
            send(b, nr + d * nh + 1, r, flip(hi, 1) * 2 + lo, own)
            send(b, nr + d * nh + 2, r, flip(hi, 2) * 2 + lo, own)
        else:
            loop(1, nh, lambda e: send(b, nr + d * nh + e, r, ((hi + e) % nh) * 2 + lo, own))
        to_partner(b, d, 0, own)

    def to_partner(b, d, e, own):
        send(b, nr + nr * nh + d * nh + e, r, hi * 2 + 1 - lo, own)

    def from_row(d):
        b = block_id(d, hi)
        arrived(b)
        to_plane(b, d, False)

    def relay(d):
        if quad:
            near = flip(hi, 1) * (1 - lo) + flip(hi, 2) * lo
            side = flip(hi, 1) * lo + flip(hi, 2) * (1 - lo)
            b = block_id(d, near)
            arrived(b)
            send(b, nr + d * nh + 3, r, side * 2 + lo, False)
            to_partner(b, d, 1, False)
            for e, high in ((2, side), (3, 3 - hi)):
                b = block_id(d, high)
                arrived(b)
                to_partner(b, d, e, False)
        else:
            def one(e):
                b = block_id(d, (hi + nh - e) % nh)
                arrived(b)
                to_partner(b, d, e, False)
            loop(1, nh, one)

    def complete(d):
        loop(0, nh, lambda e: arrived(row_from(d) * nc + e * 2 + (1 - lo)))

    to_plane(me, 0, True)
    loop(1, nr, lambda d: send(me, d, row_to(d), c, True))

    for copy in copies:
        copy.wait()
    valid = valid_ref[...]
    wide = valid.astype(jnp.float32)
    b_ref[...] = jnp.broadcast_to(-kap * jnp.sum(wide * wide, axis=1, keepdims=True), b_ref.shape)
    classes = pair_ref.shape[0]
    pair = pair_ref[...]
    table = jnp.zeros(pair.shape, jnp.float32)
    for level in range(level_ref.shape[0]):
        table = table + jnp.where(pair == level, level_ref[level], 0.0)
    table_ref[...] = jnp.zeros_like(table_ref)
    table_ref[0:classes, 0:classes] = table * (-0.5 * width)
    hot = (lax.broadcasted_iota(jnp.int32, (LANES, nv), 0) == vlab_ref[...]).astype(jnp.float32)
    hot = hot.T.astype(jnp.bfloat16)
    for k, part in enumerate(pieces(table_ref[...], 3)):
        y_ref[k] = dot(hot, part, NT).astype(jnp.bfloat16)

    chunk = 256
    per = chunk // n
    ones = jnp.ones((8, width), jnp.bfloat16)

    def build_chunk(m):
        rows = buf[pl.ds(m * per, per)].reshape(chunk, width)
        labels = jnp.concatenate([labs[m * per + q] for q in range(per)], axis=1)
        ids = lax.broadcasted_iota(jnp.int32, (LANES, chunk), 0)
        t_hot = (ids == labels).astype(jnp.float32).astype(jnp.bfloat16)
        total = dot(valid_ref[...], rows, NT)
        for k in range(3):
            total = total + dot(y_ref[k], t_hot)
        at = pl.ds(pl.multiple_of(m * chunk, chunk), chunk)
        cost[:, at] = total * (2.0 * kap)
        wide = rows.astype(jnp.float32)
        high, low = pieces(wide * wide, 2)
        sq = dot(ones, high, NT) + dot(ones, low, NT)
        norm_ref[:, at] = sq[0:1] * kap
        row_part(0, at, chunk)

    def build(d):
        here = nc * n // chunk
        loop(0, here, lambda m: build_chunk(row_from(d) * here + m))

    def row_part(e, at, span):
        def term(k):
            rows = pl.ds(pl.multiple_of(k * 8, 8), 8)
            pot = b_ref[rows, :]
            return cost[rows, at] + jnp.concatenate([pot] * (span // LANES), axis=1)

        high = lax.fori_loop(0, nv // 8, lambda k, h: jnp.maximum(h, term(k)),
                             jnp.full((8, span), -jnp.inf, jnp.float32), unroll=8)
        high = jnp.max(high, axis=0, keepdims=True)
        wide_high = jnp.broadcast_to(high, (8, span))
        total = lax.fori_loop(0, nv // 8, lambda k, s: s + jnp.exp2(term(k) - wide_high),
                              jnp.zeros((8, span), jnp.float32), unroll=8)
        total = jnp.sum(total, axis=0, keepdims=True)
        pbuf[e, c, :, at] = high + log2(total)

    if square:
        from_row(1)
        relay(0)
        from_row(2)
        relay(1)
        complete(0)
        build(0)
        from_row(3)
        relay(2)
        complete(1)
        build(1)
        relay(3)
        complete(2)
        build(2)
        complete(3)
        build(3)
    else:
        loop(1, nr, from_row)
        loop(0, nr, relay)
        loop(0, nr, complete)
        loop(0, nr, build)
    a_ref[0] = -norm_ref[...]

    full_rows = nt
    full_cols = nv * nr * nc
    span = 512

    def row_side(e):
        for w in range(nt // span):
            row_part(e, slice(w * span, (w + 1) * span), span)

    def fold(op, values):
        while len(values) > 1:
            values = [op(*values[k:k + 2]) if k + 1 < len(values) else values[k]
                      for k in range(0, len(values), 2)]
        return values[0]

    def lanes(x):
        return [x[:, k:k + LANES] for k in range(0, x.shape[1], LANES)]

    def col_side(a):
        pot = jnp.broadcast_to(a, (8, nt))

        def highest(k, _):
            rows = pl.ds(pl.multiple_of(k * 8, 8), 8)
            part_ref[rows, :] = fold(jnp.maximum, lanes(cost[rows, :] + pot))
            return 0

        lax.fori_loop(0, nv // 8, highest, 0, unroll=4)
        high_ref[...] = jnp.broadcast_to(jnp.max(part_ref[...], axis=1, keepdims=True), high_ref.shape)

        def summed(k, _):
            rows = pl.ds(pl.multiple_of(k * 8, 8), 8)
            high = high_ref[rows, :]
            part_ref[rows, :] = fold(jnp.add, [jnp.exp2(x - high) for x in lanes(cost[rows, :] + pot)])
            return 0

        lax.fori_loop(0, nv // 8, summed, 0, unroll=4)
        total = jnp.broadcast_to(jnp.sum(part_ref[...], axis=1, keepdims=True), part_ref.shape)
        b_ref[...] = 0.5 * (b_ref[...] + (math.log2(full_rows) - (high_ref[...] + log2(total))))

    def p_copy(e, d, to):
        src = c if to else (c + nc - d) % nc
        return rc(pbuf.at[e, src], pbuf.at[e, src], psend.at[e, d], precv.at[e, d], r, (c + d) % nc)

    def z_copy(e, d, to):
        src = r if to else (r + nr - d) % nr
        return rc(zbuf.at[e, src], zbuf.at[e, src], zsend.at[e, d], zrecv.at[e, d], (r + d) % nr, c)

    def joined(parts):
        high = jnp.max(parts, axis=0)
        return high + log2(jnp.sum(jnp.exp2(parts - high[None]), axis=0))

    def send_plane(e):
        loop(1, nc, lambda d: p_copy(e, d, True).start())

    def turn(e):
        loop(1, nc, lambda d: p_copy(e, d, False).wait_recv())
        zbuf[e, r] = joined(pbuf[e])
        loop(1, nr, lambda d: z_copy(e, d, True).start())

    def finish(e):
        loop(1, nr, lambda d: z_copy(e, d, False).wait_recv())
        a_ref[e + 1] = 0.5 * (a_ref[e] + (math.log2(full_cols) - joined(zbuf[e])))

    send_plane(0)
    col_side(a_ref[0])
    row_side(1)
    send_plane(1)
    for e in range(0, ITERS, 2):
        turn(e)
        turn(e + 1)
        finish(e)
        if e + 2 < ITERS:
            col_side(a_ref[e + 1])
            row_side(e + 2)
            send_plane(e + 2)
        finish(e + 1)
        if e + 3 < ITERS:
            col_side(a_ref[e + 2])
            row_side(e + 3)
            send_plane(e + 3)

    row_pot = (a_ref[ITERS] + norm_ref[...]) * (1.0 / SCALE)
    result = (row_pot * full_rows - jnp.sum(row_pot, axis=1, keepdims=True)) * (1.0 / (full_rows - 1))
    norm_ref[...] = result
    span_out = nt // nr
    out_ref[...] = norm_ref[:, pl.ds(pl.multiple_of(r * span_out, span_out), span_out)]

    loop(1, nr, sent)
    loop(0, nr, lambda d: loop(1, nh, lambda e: sent(nr + d * nh + e)))
    loop(0, nr, lambda d: loop(0, nh, lambda e: sent(nr + nr * nh + d * nh + e)))
    for e in range(ITERS):
        loop(1, nc, lambda d: p_copy(e, d, True).wait_send())
        loop(1, nr, lambda d: z_copy(e, d, True).wait_send())


def solution(mesh):
    nr, nc = mesh.shape["row"], mesh.shape["col"]

    def shards(train_embed, valid_embed, train_labels, valid_labels, pair_level, level_cost):
        n, width = train_embed.shape
        nv = valid_embed.shape[0]
        nt = nr * nc * n
        vmem = pl.BlockSpec(memory_space=pltpu.VMEM)
        dma = pltpu.SemaphoreType.DMA
        sends = nr + nr * nc
        out = pl.pallas_call(
            functools.partial(kernel, nr, nc, n),
            out_shape=jax.ShapeDtypeStruct((1, nt // nr), jnp.float32),
            in_specs=[pl.BlockSpec(memory_space=pl.ANY)] * 6,
            out_specs=vmem,
            scratch_shapes=[
                pltpu.VMEM((nr * nc, n, width), jnp.bfloat16),
                pltpu.VMEM((nr * nc, 1, n), jnp.int32),
                pltpu.SMEM(level_cost.shape, jnp.float32),
                pltpu.VMEM(pair_level.shape, jnp.int32),
                pltpu.VMEM((nv, width), jnp.bfloat16),
                pltpu.VMEM((1, nv), jnp.int32),
                pltpu.VMEM((nv, nt), jnp.float32),
                pltpu.VMEM((3, nv, LANES), jnp.bfloat16),
                pltpu.VMEM((nv, LANES), jnp.float32),
                pltpu.VMEM((ITERS + 1, 1, nt), jnp.float32),
                pltpu.VMEM((1, nt), jnp.float32),
                pltpu.VMEM((LANES, LANES), jnp.float32),
                pltpu.VMEM((nv, LANES), jnp.float32),
                pltpu.VMEM((nv, LANES), jnp.float32),
                pltpu.VMEM((ITERS, nc, 1, nt), jnp.float32),
                pltpu.VMEM((ITERS, nr, 1, nt), jnp.float32),
                dma((6,)), dma((sends,)), dma((sends,)), dma((nr * nc,)), dma((nr * nc,)),
                dma((ITERS, nc)), dma((ITERS, nc)), dma((ITERS, nr)), dma((ITERS, nr)),
            ],
            compiler_params=pltpu.CompilerParams(
                collective_id=0, has_side_effects=True, vmem_limit_bytes=56 * 1024 * 1024),
            name="sinkhorn",
        )(level_cost, pair_level, train_embed, train_labels[None, :], valid_embed, valid_labels[None, :])
        return out.reshape(nt // nr)

    placed = (
        P(("row", "col"), None),
        P(("row", "col"), None),
        P(("row", "col")),
        P(("row", "col")),
        P(),
        P(),
    )
    return jax.shard_map(shards, mesh=mesh, in_specs=placed, out_specs=P("row"), check_vma=False)
```

time: 54.3 us -> 55.2 us (1.017)
  Pallas kernels: 50.7 us -> 53.7 us
  other arithmetic: 1.38 us -> 0 us
  local copies, waits for them, and re-layouts: 1.99 us -> 1.26 us
    pallas_call x1, Pallas kernels: 50.7 us -> 53.7 us  [shards(): pl.pallas_call(functools.partial(kernel, nr, nc, n), out_shape=jax.ShapeD...]
    concatenate x1 -> x0, other arithmetic: 1.38 us -> none  [shards(): jnp.concatenate([train_embed, jnp.broadcast_to(labels, (16, width))], axi...]
    unnamed x3 -> x1, local copies, waits for them, and re-layouts: 1.89 us -> 1.26 us
where the time goes in v2:
time: 55.2 us; the launch traced here: 55 us
  Pallas kernels  53.7 us (97%)
  local copies, waits for them, and re-layouts  1.26 us (2%)
    pallas_call x1, Pallas kernels, shards(): pl.pallas_call(functools.partial(kernel, nr, nc, n), out_shape=jax.ShapeD...  53.7 us
    unnamed x1, local copies, waits for them, and re-layouts  1.26 us

profile of v2, /device:TPU:0, one launch (start us, length us, event | category | flops | bytes accessed | tf_op | source)
XLA Modules:
  0.0 55.0 jit_solution(11650687469541040564)
XLA Ops:
  0.0 53.7 %sinkhorn.1 = f32[1,512]{1,0:T(1,128)} custom-call(f32[4]{0:T(128)} %level_hbm.1, s32[100,100]{1,0:T(8,128)} %pair_hbm.1, bf16[64,256]{1,0:T(8,128)(2,1)} %block_ref.1, s32[1,64]{1,0:T(1,128)} %bitcast.5, bf16[512,256]{1,0:T(8,128)(2,1)} %valid_hbm.1, s32[1,512]{1,0:T(1,128)} %bitcast.4), custom_call_target="tpu_custom_call" | custom-call | tf_op jit(solution)/shard_map/sinkhorn/pallas_call | solution.py:331
  53.7 1.3 %copy.8 = f32[512]{0:T(512)} copy(f32[512]{0:T(512)} %bitcast.3) | data formatting | bytes 4096

commit v3 on v2

--- a/solution.py
+++ b/solution.py
@@ -33,8 +33,8 @@
     return lax.dot_general(a, b, dims, preferred_element_type=jnp.float32)
 
 
-def kernel(nr, nc, n, level_hbm, pair_hbm, block_ref, lab_ref, valid_hbm, vlab_hbm, out_ref,
-           buf, labs, level_ref, pair_ref, valid_ref, vlab_ref,
+def kernel(nr, nc, n, level_hbm, pair_hbm, block_ref, lab_hbm, valid_hbm, vlab_hbm, out_ref,
+           buf, labs, lab_ref, level_ref, pair_ref, valid_ref, vlab_ref,
            cost, y_ref, b_ref, a_ref, norm_ref, table_ref, part_ref, high_ref, pbuf, zbuf,
            local_sem, gsend, lsend, grecv, lrecv, psend, precv, zsend, zrecv):
     width = valid_ref.shape[1]
@@ -61,7 +61,7 @@
             lax.fori_loop(lower, upper, lambda i, _: (body(i), 0)[1], 0)
 
     pairs = ((level_hbm, level_ref), (pair_hbm, pair_ref), (valid_hbm, valid_ref), (vlab_hbm, vlab_ref),
-             (block_ref, buf.at[me]), (lab_ref, labs.at[me]))
+             (block_ref, buf.at[me]), (lab_hbm, lab_ref))
     copies = [pltpu.make_async_copy(src, dst, local_sem.at[k]) for k, (src, dst) in enumerate(pairs)]
     for copy in copies:
         copy.start()
@@ -71,10 +71,16 @@
         barrier, inc=1, device_id={"row": (r + d) % nr, "col": c}, device_id_type=pl.DeviceIdType.MESH))
     loop(1, nc, lambda d: pl.semaphore_signal(
         barrier, inc=1, device_id={"row": r, "col": (c + d) % nc}, device_id_type=pl.DeviceIdType.MESH))
+    for copy in copies[4:]:
+        copy.wait()
+    wide = buf[me].astype(jnp.float32)
+    wide = jnp.sum(wide * wide, axis=1, keepdims=True) * kap
+    mine = lax.broadcasted_iota(jnp.int32, (n, n), 0) == lax.broadcasted_iota(jnp.int32, (n, n), 1)
+    labs[me, 0:1, :] = lab_ref[...].astype(jnp.float32)
+    labs[me, 1:2, :] = jnp.sum(jnp.where(mine, wide, 0.0), axis=0, keepdims=True)
     pl.semaphore_wait(barrier, nr + nc - 2)
 
     square = nr == 4
-    quad = nh == 4
 
     def flip(x, k):
         if k == 1:
@@ -89,13 +95,13 @@
 
     def send(b, k, row, col, own):
         data = rc(block_ref if own else buf.at[b], buf.at[b], gsend.at[k], grecv.at[b], row, col)
-        label = rc(lab_ref if own else labs.at[b], labs.at[b], lsend.at[k], lrecv.at[b], row, col)
+        label = rc(labs.at[b], labs.at[b], lsend.at[k], lrecv.at[b], row, col)
         data.start()
         label.start()
 
     def sent(k):
         rc(block_ref, buf.at[me], gsend.at[k], grecv.at[me], r, hi * 2 + 1 - lo).wait_send()
-        rc(lab_ref, labs.at[me], lsend.at[k], lrecv.at[me], r, hi * 2 + 1 - lo).wait_send()
+        rc(labs.at[me], labs.at[me], lsend.at[k], lrecv.at[me], r, hi * 2 + 1 - lo).wait_send()
 
     def arrived(b):
         rc(buf.at[b], buf.at[b], gsend.at[0], grecv.at[b], r, hi * 2 + 1 - lo).wait_recv()
@@ -105,11 +111,7 @@
         return row_from(d) * nc + high * 2 + lo
 
     def to_plane(b, d, own):
-        if quad:
-            send(b, nr + d * nh + 1, r, flip(hi, 1) * 2 + lo, own)
-            send(b, nr + d * nh + 2, r, flip(hi, 2) * 2 + lo, own)
-        else:
-            loop(1, nh, lambda e: send(b, nr + d * nh + e, r, ((hi + e) % nh) * 2 + lo, own))
+        loop(1, nh, lambda e: send(b, nr + d * nh + e, r, ((hi + e) % nh) * 2 + lo, own))
         to_partner(b, d, 0, own)
 
     def to_partner(b, d, e, own):
@@ -121,23 +123,11 @@
         to_plane(b, d, False)
 
     def relay(d):
-        if quad:
-            near = flip(hi, 1) * (1 - lo) + flip(hi, 2) * lo
-            side = flip(hi, 1) * lo + flip(hi, 2) * (1 - lo)
-            b = block_id(d, near)
+        def one(e):
+            b = block_id(d, (hi + nh - e) % nh)
             arrived(b)
-            send(b, nr + d * nh + 3, r, side * 2 + lo, False)
-            to_partner(b, d, 1, False)
-            for e, high in ((2, side), (3, 3 - hi)):
-                b = block_id(d, high)
-                arrived(b)
-                to_partner(b, d, e, False)
-        else:
-            def one(e):
-                b = block_id(d, (hi + nh - e) % nh)
-                arrived(b)
-                to_partner(b, d, e, False)
-            loop(1, nh, one)
+            to_partner(b, d, e, False)
+        loop(1, nh, one)
 
     def complete(d):
         loop(0, nh, lambda e: arrived(row_from(d) * nc + e * 2 + (1 - lo)))
@@ -145,7 +135,7 @@
     to_plane(me, 0, True)
     loop(1, nr, lambda d: send(me, d, row_to(d), c, True))
 
-    for copy in copies:
+    for copy in copies[:4]:
         copy.wait()
     valid = valid_ref[...]
     wide = valid.astype(jnp.float32)
@@ -160,31 +150,31 @@
     hot = (lax.broadcasted_iota(jnp.int32, (LANES, nv), 0) == vlab_ref[...]).astype(jnp.float32)
     hot = hot.T.astype(jnp.bfloat16)
     for k, part in enumerate(pieces(table_ref[...], 3)):
-        y_ref[k] = dot(hot, part, NT).astype(jnp.bfloat16)
+        y_ref[:, k * LANES:(k + 1) * LANES] = dot(hot, part, NT).astype(jnp.bfloat16)
 
     chunk = 256
     per = chunk // n
-    ones = jnp.ones((8, width), jnp.bfloat16)
 
     def build_chunk(m):
         rows = buf[pl.ds(m * per, per)].reshape(chunk, width)
         labels = jnp.concatenate([labs[m * per + q] for q in range(per)], axis=1)
         ids = lax.broadcasted_iota(jnp.int32, (LANES, chunk), 0)
-        t_hot = (ids == labels).astype(jnp.float32).astype(jnp.bfloat16)
-        total = dot(valid_ref[...], rows, NT)
-        for k in range(3):
-            total = total + dot(y_ref[k], t_hot)
+        t_hot = (ids == labels[0:1].astype(jnp.int32)).astype(jnp.float32).astype(jnp.bfloat16)
+        total = dot(valid_ref[...], rows, NT) + dot(y_ref[...], jnp.concatenate([t_hot] * 3, axis=0))
         at = pl.ds(pl.multiple_of(m * chunk, chunk), chunk)
         cost[:, at] = total * (2.0 * kap)
-        wide = rows.astype(jnp.float32)
-        high, low = pieces(wide * wide, 2)
-        sq = dot(ones, high, NT) + dot(ones, low, NT)
-        norm_ref[:, at] = sq[0:1] * kap
-        row_part(0, at, chunk)
+        norm_ref[:, at] = labels[1:2]
 
     def build(d):
         here = nc * n // chunk
         loop(0, here, lambda m: build_chunk(row_from(d) * here + m))
+        row_part(0, pl.ds(pl.multiple_of(row_from(d) * here * chunk, chunk), here * chunk), here * chunk)
+
+    def fold(op, values):
+        while len(values) > 1:
+            values = [op(*values[k:k + 2]) if k + 1 < len(values) else values[k]
+                      for k in range(0, len(values), 2)]
+        return values[0]
 
     def row_part(e, at, span):
         def term(k):
@@ -192,23 +182,28 @@
             pot = b_ref[rows, :]
             return cost[rows, at] + jnp.concatenate([pot] * (span // LANES), axis=1)
 
-        high = lax.fori_loop(0, nv // 8, lambda k, h: jnp.maximum(h, term(k)),
-                             jnp.full((8, span), -jnp.inf, jnp.float32), unroll=8)
-        high = jnp.max(high, axis=0, keepdims=True)
+        def sweep(op, start, value):
+            step = math.gcd(nv // 8, 8)
+
+            def body(k, state):
+                return op(state, fold(op, [value(k * step + q) for q in range(step)]))
+
+            return lax.fori_loop(0, nv // 8 // step, body, jnp.full((8, span), start, jnp.float32), unroll=2)
+
+        high = jnp.max(sweep(jnp.maximum, -jnp.inf, term), axis=0, keepdims=True)
         wide_high = jnp.broadcast_to(high, (8, span))
-        total = lax.fori_loop(0, nv // 8, lambda k, s: s + jnp.exp2(term(k) - wide_high),
-                              jnp.zeros((8, span), jnp.float32), unroll=8)
+        total = sweep(jnp.add, 0.0, lambda k: jnp.exp2(term(k) - wide_high))
         total = jnp.sum(total, axis=0, keepdims=True)
         pbuf[e, c, :, at] = high + log2(total)
 
     if square:
         from_row(1)
+        from_row(2)
         relay(0)
-        from_row(2)
+        from_row(3)
         relay(1)
         complete(0)
         build(0)
-        from_row(3)
         relay(2)
         complete(1)
         build(1)
@@ -231,12 +226,6 @@
     def row_side(e):
         for w in range(nt // span):
             row_part(e, slice(w * span, (w + 1) * span), span)
-
-    def fold(op, values):
-        while len(values) > 1:
-            values = [op(*values[k:k + 2]) if k + 1 < len(values) else values[k]
-                      for k in range(0, len(values), 2)]
-        return values[0]
 
     def lanes(x):
         return [x[:, k:k + LANES] for k in range(0, x.shape[1], LANES)]
@@ -335,13 +324,14 @@
             out_specs=vmem,
             scratch_shapes=[
                 pltpu.VMEM((nr * nc, n, width), jnp.bfloat16),
-                pltpu.VMEM((nr * nc, 1, n), jnp.int32),
+                pltpu.VMEM((nr * nc, 2, n), jnp.float32),
+                pltpu.VMEM((1, n), jnp.int32),
                 pltpu.SMEM(level_cost.shape, jnp.float32),
                 pltpu.VMEM(pair_level.shape, jnp.int32),
                 pltpu.VMEM((nv, width), jnp.bfloat16),
                 pltpu.VMEM((1, nv), jnp.int32),
                 pltpu.VMEM((nv, nt), jnp.float32),
-                pltpu.VMEM((3, nv, LANES), jnp.bfloat16),
+                pltpu.VMEM((nv, 3 * LANES), jnp.bfloat16),
                 pltpu.VMEM((nv, LANES), jnp.float32),
                 pltpu.VMEM((ITERS + 1, 1, nt), jnp.float32),
                 pltpu.VMEM((1, nt), jnp.float32),

time: 55.2 us -> 40.8 us (0.74)
  Pallas kernels: 53.7 us -> 39.4 us
    pallas_call x1, Pallas kernels: 53.7 us -> 39.4 us  [shards(): pl.pallas_call(functools.partial(kernel, nr, nc, n), out_shape=jax.ShapeD...]
where the time goes in v3:
time: 40.8 us; the launch traced here: 40.6 us
  Pallas kernels  39.4 us (97%)
  local copies, waits for them, and re-layouts  1.26 us (3%)
    pallas_call x1, Pallas kernels, shards(): pl.pallas_call(functools.partial(kernel, nr, nc, n), out_shape=jax.ShapeD...  39.4 us
    unnamed x1, local copies, waits for them, and re-layouts  1.26 us

profile of v3, /device:TPU:0, one launch (start us, length us, event | category | flops | bytes accessed | tf_op | source)
XLA Modules:
  0.0 40.6 jit_solution(4528114358231850374)
XLA Ops:
  0.0 39.4 %sinkhorn.1 = f32[1,512]{1,0:T(1,128)} custom-call(f32[4]{0:T(128)} %level_hbm.1, s32[100,100]{1,0:T(8,128)} %pair_hbm.1, bf16[64,256]{1,0:T(8,128)(2,1)} %block_ref.1, s32[1,64]{1,0:T(1,128)} %bitcast.5, bf16[512,256]{1,0:T(8,128)(2,1)} %valid_hbm.1, s32[1,512]{1,0:T(1,128)} %bitcast.4), custom_call_target="tpu_custom_call" | custom-call | tf_op jit(solution)/shard_map/sinkhorn/pallas_call | solution.py:320
  39.4 1.3 %copy.8 = f32[512]{0:T(512)} copy(f32[512]{0:T(512)} %bitcast.3) | data formatting | bytes 4096

commit v4 on v3

--- a/solution.py
+++ b/solution.py
@@ -319,7 +319,7 @@
         sends = nr + nr * nc
         out = pl.pallas_call(
             functools.partial(kernel, nr, nc, n),
-            out_shape=jax.ShapeDtypeStruct((1, nt // nr), jnp.float32),
+            out_shape=pltpu.VMEM((1, nt // nr), jnp.float32),
             in_specs=[pl.BlockSpec(memory_space=pl.ANY)] * 6,
             out_specs=vmem,
             scratch_shapes=[

time: 40.8 us -> 39.5 us (0.968)
  local copies, waits for them, and re-layouts: 1.26 us -> 0.58 us
  Pallas kernels: 39.4 us -> 38.8 us
    unnamed x1, local copies, waits for them, and re-layouts: 1.26 us -> 0.58 us
    pallas_call x1, Pallas kernels: 39.4 us -> 38.8 us  [shards(): pl.pallas_call(functools.partial(kernel, nr, nc, n), out_shape=pltpu.VMEM...]
where the time goes in v4:
time: 39.5 us; the launch traced here: 39.4 us
  Pallas kernels  38.8 us (98%)
  local copies, waits for them, and re-layouts  0.58 us (1%)
    pallas_call x1, Pallas kernels, shards(): pl.pallas_call(functools.partial(kernel, nr, nc, n), out_shape=pltpu.VMEM...  38.8 us

profile of v4, /device:TPU:0, one launch (start us, length us, event | category | flops | bytes accessed | tf_op | source)
XLA Modules:
  0.0 39.4 jit_solution(4133352446190486520)
XLA Ops:
  0.0 38.8 %sinkhorn.1 = f32[1,512]{1,0:T(1,128)S(1)} custom-call(f32[4]{0:T(128)} %level_hbm.1, s32[100,100]{1,0:T(8,128)} %pair_hbm.1, bf16[64,256]{1,0:T(8,128)(2,1)} %block_ref.1, s32[1,64]{1,0:T(1,128)} %bitcast.5, bf16[512,256]{1,0:T(8,128)(2,1)} %valid_hbm.1, s32[1,512]{1,0:T(1,128)} %bitcast.4), custom_call_target="tpu_custom_call" | custom-call | tf_op jit(solution)/shard_map/sinkhorn/pallas_call | solution.py:320
  38.8 0.6 %copy.8 = f32[512]{0:T(512)} copy(f32[512]{0:T(512)S(1)} %bitcast.3) | data formatting | bytes 4096

commit v5 on v4

--- a/solution.py
+++ b/solution.py
@@ -221,7 +221,7 @@
 
     full_rows = nt
     full_cols = nv * nr * nc
-    span = 512
+    span = math.gcd(nt, 1024)
 
     def row_side(e):
         for w in range(nt // span):

time: 39.5 us -> 39.2 us (level)
  no operation moved by 1% of the time
where the time goes in v5:
time: 39.2 us; the launch traced here: 39.1 us
  Pallas kernels  38.5 us (98%)
  local copies, waits for them, and re-layouts  0.58 us (1%)
    pallas_call x1, Pallas kernels, shards(): pl.pallas_call(functools.partial(kernel, nr, nc, n), out_shape=pltpu.VMEM...  38.5 us

profile of v5, /device:TPU:0, one launch (start us, length us, event | category | flops | bytes accessed | tf_op | source)
XLA Modules:
  0.0 39.1 jit_solution(8653580622470039781)
XLA Ops:
  0.0 38.5 %sinkhorn.1 = f32[1,512]{1,0:T(1,128)S(1)} custom-call(f32[4]{0:T(128)} %level_hbm.1, s32[100,100]{1,0:T(8,128)} %pair_hbm.1, bf16[64,256]{1,0:T(8,128)(2,1)} %block_ref.1, s32[1,64]{1,0:T(1,128)} %bitcast.5, bf16[512,256]{1,0:T(8,128)(2,1)} %valid_hbm.1, s32[1,512]{1,0:T(1,128)} %bitcast.4), custom_call_target="tpu_custom_call" | custom-call | tf_op jit(solution)/shard_map/sinkhorn/pallas_call | solution.py:320
  38.5 0.6 %copy.8 = f32[512]{0:T(512)} copy(f32[512]{0:T(512)S(1)} %bitcast.3) | data formatting | bytes 4096
